TPU v7x, 32 devices: a whole 2x2x4 slice. The times are simulated.
32 devices in a mesh: frame: 16 (over z, x, core), head: 2 (over y).
Axes of the slice: x: 2, y: 2, z: 4, core: 2. Of those that a mesh axis runs over, the one named last changes fastest.
Arguments:
- activations: bfloat16 [32, 128, 4096], P('frame'), may hold values from -6 to 6
- w_query: bfloat16 [4096, 4096], P('frame', 'head'), may hold values from -0.09375 to 0.09375
- w_key: bfloat16 [4096, 4096], P('frame', 'head'), may hold values from -0.09375 to 0.09375
- w_value: bfloat16 [4096, 4096], P('frame', 'head'), may hold values from -0.09375 to 0.09375
- q_gain: float32 [128], replicated, may hold values from 0.1 to 1.9
- k_gain: float32 [128], replicated, may hold values from 0.1 to 1.9
- grad_attn: bfloat16 [32, 128, 4096], P('frame', None, 'head'), may hold values from -6 to 6
Outputs:
- grad_input: bfloat16 [32, 128, 4096], P('frame', None, 'head')
- grad_wq: float32 [4096, 4096], P('frame', 'head')
- grad_wk: float32 [4096, 4096], P('frame', 'head')
- grad_wv: float32 [4096, 4096], P('frame', 'head')
All inputs are finite; a program needn't handle non-finite values.
Results may differ from a plain program's by a relative error of at most 0.018.
Values may be sent and summed in bfloat16 or wider, within the bound.
A program may use at most 192 MiB of HBM per device.

v0:
```python
import math

import jax
import jax.numpy as jnp
from jax import lax
from jax.sharding import Mesh, PartitionSpec as P

HD = 128


epsilon = 1e-06


def scaled(raw, gain):
    inverse = lax.rsqrt(jnp.mean(raw * raw, axis=-1, keepdims=True) + epsilon)
    return raw * inverse * gain


def attend(query, key_norm, value):
    factor = 1.0 / math.sqrt(query.shape[-1])
    scores = jnp.einsum("fphd,gphd->phfg", query, key_norm) * factor
    expon = jnp.exp(scores)
    weights = expon / jnp.sum(expon, axis=-1, keepdims=True)
    return jnp.einsum("phfg,gphd->fphd", weights, value)


def attend_back(query, key_norm, value, cotan):
    _, pull = jax.vjp(
        attend, query.astype(jnp.float32), key_norm.astype(jnp.float32), value.astype(jnp.float32)
    )
    grads = pull(cotan.astype(jnp.float32))
    return (
        grads[0].astype(jnp.bfloat16),
        grads[1].astype(jnp.bfloat16),
        grads[2].astype(jnp.bfloat16),
    )


def line_split(n_frame, heads_here):
    part = 1
    while (
        4 * part * part <= n_frame
        and n_frame % (2 * part) == 0
        and heads_here % (2 * part) == 0
    ):
        part *= 2
    return part


def make_body(n_a, n_b):
    def body(activations, w_query, w_key, w_value, q_gain, k_gain, grad_attn):
        frames_here, patches, width = activations.shape
        rows_here, head_cols = w_query.shape
        cols = head_cols // n_a
        heads = cols // HD
        frames = frames_here * n_a
        tokens = frames * patches

        def stacked(x):
            return jnp.concatenate([x[:, i * cols : (i + 1) * cols] for i in range(n_a)], axis=0)

        def exchange(x):
            return lax.all_to_all(x, "fa", split_axis=0, concat_axis=0, tiled=True)

        acts = lax.all_gather(activations.reshape(-1, width), "fa", axis=0, tiled=True)
        cotan = exchange(stacked(grad_attn.reshape(-1, head_cols)))
        acts, cotan, *mine = lax.optimization_barrier(
            (acts, cotan, exchange(stacked(w_query)), stacked(w_key), stacked(w_value))
        )
        mine[1:] = [exchange(m) for m in mine[1:]]
        wq, wk, wv = (lax.all_gather(m, "fb", axis=0, tiled=True) for m in mine)

        def blocks(x, order):
            return jnp.concatenate(
                [x[:, i * rows_here : (i + 1) * rows_here] for i in order], axis=1
            )

        rows = blocks(acts, [i * n_b + j for j in range(n_b) for i in range(n_a)])

        def spread(x):
            return lax.all_to_all(x, "fb", split_axis=1, concat_axis=0, tiled=True)

        def back(x):
            return lax.all_to_all(x, "fb", split_axis=0, concat_axis=1, tiled=True)

        shape4 = (frames, patches, heads, HD)
        cotan = spread(cotan.reshape(shape4))

        q_raw = jnp.dot(rows, wq, preferred_element_type=jnp.float32).reshape(tokens, heads, HD)
        q_norm = spread(scaled(q_raw, q_gain).astype(jnp.bfloat16).reshape(shape4))
        k_raw = jnp.dot(rows, wk, preferred_element_type=jnp.float32).reshape(tokens, heads, HD)
        k_norm = spread(scaled(k_raw, k_gain).astype(jnp.bfloat16).reshape(shape4))
        value = jnp.dot(rows, wv, preferred_element_type=jnp.float32)
        value = spread(value.astype(jnp.bfloat16).reshape(shape4))

        grads = attend_back(q_norm, k_norm, value, cotan)
        d_val, d_qn, d_kn = back(grads[2]), back(grads[0]), back(grads[1])

        _, pull_query = jax.vjp(lambda raw: scaled(raw, q_gain), q_raw)
        _, pull_key = jax.vjp(lambda raw: scaled(raw, k_gain), k_raw)
        d_q = pull_query(d_qn.reshape(tokens, heads, HD).astype(jnp.float32))[0]
        d_q = d_q.astype(jnp.bfloat16).reshape(tokens, cols)
        d_k = pull_key(d_kn.reshape(tokens, heads, HD).astype(jnp.float32))[0]
        d_k = d_k.astype(jnp.bfloat16).reshape(tokens, cols)
        d_v = d_val.reshape(tokens, cols)

        def weight_grad(d):
            term = lax.dot_general(
                rows, d, (((0,), (0,)), ((), ())), preferred_element_type=jnp.float32
            ).astype(jnp.bfloat16)
            return lax.psum_scatter(term, "fb", scatter_dimension=0, tiled=True)

        def regroup(summed):
            out = exchange(summed)
            out = [out[i * rows_here : (i + 1) * rows_here] for i in range(n_a)]
            return jnp.concatenate(out, axis=1).astype(jnp.float32)

        sum_v, sum_q, sum_k = weight_grad(d_v), weight_grad(d_q), weight_grad(d_k)

        contract = (((1,), (1,)), ((), ()))
        partial = lax.dot_general(d_q, wq, contract, preferred_element_type=jnp.float32)
        partial = partial + lax.dot_general(d_k, wk, contract, preferred_element_type=jnp.float32)
        partial = partial + lax.dot_general(d_v, wv, contract, preferred_element_type=jnp.float32)
        partial = blocks(
            partial.astype(jnp.bfloat16), [j * n_a + i for i in range(n_a) for j in range(n_b)]
        )
        partial, sum_q, sum_k, sum_v = lax.optimization_barrier((partial, sum_q, sum_k, sum_v))
        partial = lax.psum_scatter(partial, "head", scatter_dimension=1, tiled=True)
        sums = (regroup(sum_q), regroup(sum_k), regroup(sum_v))
        partial, sums = lax.optimization_barrier((partial, sums))
        grad_input = lax.psum_scatter(partial, "fa", scatter_dimension=0, tiled=True)
        grad_input = grad_input.reshape(frames_here, patches, -1)
        return (grad_input, *sums)

    return body


def solution(mesh):
    n_frame, n_head = mesh.shape["frame"], mesh.shape["head"]

    def run(activations, w_query, w_key, w_value, q_gain, k_gain, grad_attn):
        n_a = line_split(n_frame, w_query.shape[1] // (HD * n_head))
        n_b = n_frame // n_a
        split = Mesh(mesh.devices.reshape(n_a, n_b, n_head), ("fa", "fb", "head"))
        frame = ("fa", "fb")
        placed = (
            P(frame, None, None),
            P(frame, "head"),
            P(frame, "head"),
            P(frame, "head"),
            P(),
            P(),
            P(frame, None, "head"),
        )
        return jax.shard_map(
            make_body(n_a, n_b),
            mesh=split,
            in_specs=placed,
            out_specs=(
                P(frame, None, "head"),
                P(frame, "head"),
                P(frame, "head"),
                P(frame, "head"),
            ),
            check_vma=False,
        )(activations, w_query, w_key, w_value, q_gain, k_gain, grad_attn)

    return run
```

profile of v0, /device:TPU:16, one launch (start us, length us, event | category | flops | bytes accessed | tf_op | source)
XLA Modules:
  0.0 742.7 jit_solution(7648525101042112511)
XLA Ops:
  10.7 5.3 all-to-all-start
  17.1 49.1 %all-to-all-done = bf16[4,256,512]{1,2,0:T(8,128)(2,1)S(1)} async-done(((bf16[4,256,512]{1,2,0:T(8,128)(2,1)}), bf16[4,256,512]{1,2,0:T(8,128)(2,1)S(1)}, u32[]{:S(2)}, u32[]{:S(2)}) %all-to-all-start) | async-done | bytes 1048608 | tf_op jit(solution)/shard_map/all_to_all | solution.py:63
  66.2 6.8 all-to-all-start.1
  76.4 41.9 %all-to-all-done.1 = bf16[4,256,512]{2,1,0:T(8,128)(2,1)S(1)} async-done(((bf16[4,256,512]{2,1,0:T(8,128)(2,1)}), bf16[4,256,512]{2,1,0:T(8,128)(2,1)S(1)}, u32[]{:S(2)}, u32[]{:S(2)}) %all-to-all-start.1) | async-done | bytes 1048608 | tf_op jit(solution)/shard_map/all_to_all | solution.py:63
  118.3 77.7 %all-gather.5.cloned.1.call-done = bf16[1024,4096]{1,0:T(8,128)(2,1)} async-done(((bf16[256,4096]{1,0:T(8,128)(2,1)}), bf16[1024,4096]{1,0:T(8,128)(2,1)}) %all-gather.5.cloned.1.call-update) | async-done | bytes 8388624 | tf_op jit(solution)/shard_map/all_gather | solution.py:65
  196.1 31.4 %all_to_all.180 = bf16[4,256,512]{2,1,0:T(8,128)(2,1)} all-to-all(bf16[4,256,512]{2,1,0:T(8,128)(2,1)} %bitcast.212), channel_id=1, replica_groups=mesh['fa'=4,'fb'=4,'head'=2] {'fa'}, dimensions={0} | all-to-all | bytes 2097152 | tf_op jit(solution)/shard_map/all_to_all | solution.py:63
  227.5 6.2 all-to-all-start.3
  233.7 1.9 slice_dynamic-update-slice_fusion.31
  235.7 2.0 slice_dynamic-update-slice_fusion.30
  237.9 2.2 copy.107
  240.1 1.9 slice_dynamic-update-slice_fusion.29
  242.0 1.9 slice_dynamic-update-slice_fusion.28
  244.0 2.0 slice_dynamic-update-slice_fusion.27
  245.9 1.9 slice_dynamic-update-slice_fusion.26
  251.7 4.1 all-to-all-done.3
  255.8 3.5 all-to-all-start.2
  265.6 2.0 slice_dynamic-update-slice_fusion.20
  275.2 8.3 %multiply_reduce_fusion.2 = (f32[1024,4]{0,1:T(4,128)S(1)}, f32[1024,512]{0,1:T(8,128)S(1)}) fusion(bf16[1024,4096]{1,0:T(8,128)(2,1)} %slice_dynamic-update-slice_fusion.16, bf16[4096,512]{1,0:T(8,128)(2,1)} %all-gather.9.cloned.1.call-done), kind=kOutput, calls=%fused_computation.30 | convolution fusion | flops 4296011776 | bytes 14696448 | tf_op jit(solution)/shard_map/dot_general | solution.py:89
  286.6 4.8 copy.113
  291.4 3.3 multiply_convert_fusion.1
  294.7 4.5 all-to-all-start.5
  299.3 8.3 %multiply_reduce_fusion.1 = (f32[1024,4]{0,1:T(4,128)S(1)}, f32[1024,512]{0,1:T(8,128)S(1)}) fusion(bf16[1024,4096]{1,0:T(8,128)(2,1)} %slice_dynamic-update-slice_fusion.16, bf16[4096,512]{1,0:T(8,128)(2,1)} %all-gather.11.cloned.1.call-done), kind=kOutput, calls=%fused_computation.28 | convolution fusion | flops 4296011776 | bytes 14696448 | tf_op jit(solution)/shard_map/dot_general | solution.py:91
  310.5 4.6 copy.117
  315.1 3.3 multiply_convert_fusion
  318.4 4.4 all-to-all-done.5
  322.7 4.3 all-to-all-start.7
  327.0 10.0 %convolution_convert_fusion.3 = bf16[1024,512]{1,0:T(8,128)(2,1)} fusion(bf16[1024,4096]{1,0:T(8,128)(2,1)} %slice_dynamic-update-slice_fusion.16, bf16[4096,512]{1,0:T(8,128)(2,1)} %all-gather.7.cloned.1.call-done), kind=kOutput, calls=%fused_computation.31 | convolution fusion | flops 4295491584 | bytes 13631488 | tf_op jit(solution)/shard_map/dot_general | solution.py:93
  337.1 2.1 reshape.161
  339.2 2.6 copy.110
  341.8 4.8 all-to-all-start.4
  348.2 2.0 copy.118
  350.2 4.0 fusion.44
  354.2 6.8 all-to-all-done.4
  361.0 2.8 multiply_reduce_fusion
  366.6 4.3 all-to-all-start.8
  371.1 2.9 copy.126
  374.0 11.4 %all-to-all-done.8 = bf16[32,32,4,128]{3,2,1,0:T(4,128)(2,1)} async-done(((bf16[32,32,4,128]{3,2,1,0:T(4,128)(2,1)}), bf16[32,32,4,128]{3,2,1,0:T(4,128)(2,1)}, u32[]{:S(2)}, u32[]{:S(2)}) %all-to-all-start.8) | async-done | bytes 1048608 | tf_op jit(solution)/shard_map/all_to_all | solution.py:84
  391.3 2.9 copy.124
  394.2 2.7 fusion
  397.9 9.8 %convolution_convert_fusion.2 = bf16[4096,512]{1,0:T(8,128)(2,1)} fusion(bf16[1024,4096]{1,0:T(8,128)(2,1)} %slice_dynamic-update-slice_fusion.16, bf16[1024,512]{0,1:T(8,128)(2,1)S(1)} %fusion), kind=kOutput, calls=%fused_computation.3 | convolution fusion | flops 4297064448 | bytes 13631488 | tf_op jit(solution)/shard_map/dot_general | solution.py:108
  407.7 2.0 fusion.13
  410.3 17.1 %all_to_all.181 = bf16[32,32,4,128]{3,2,1,0:T(4,128)(2,1)S(1)} all-to-all(bf16[32,32,4,128]{3,2,1,0:T(4,128)(2,1)S(1)} %copy.133), channel_id=1, replica_groups=mesh['fa'=4,'fb'=4,'head'=2] {'fb'}, dimensions={0} | all-to-all | bytes 2097152 | tf_op jit(solution)/shard_map/all_to_all | solution.py:84
  427.8 9.8 %convolution_convert_fusion = bf16[4096,512]{1,0:T(8,128)(2,1)} fusion(bf16[1024,4096]{1,0:T(8,128)(2,1)} %slice_dynamic-update-slice_fusion.16, bf16[128,8,4,128]{3,2,1,0:T(4,128)(2,1)S(1)} %bitcast.197), kind=kOutput, calls=%fused_computation.1 | convolution fusion | flops 4297064448 | bytes 13631488 | tf_op jit(solution)/shard_map/dot_general | solution.py:108
  437.6 3.6 fusion.12
  442.7 4.3 all-to-all-start.9
  448.8 13.5 %all-to-all-done.9 = bf16[32,32,4,128]{3,2,1,0:T(4,128)(2,1)} async-done(((bf16[32,32,4,128]{3,2,1,0:T(4,128)(2,1)}), bf16[32,32,4,128]{3,2,1,0:T(4,128)(2,1)}, u32[]{:S(2)}, u32[]{:S(2)}) %all-to-all-start.9) | async-done | bytes 1048608 | tf_op jit(solution)/shard_map/all_to_all | solution.py:84
  468.8 2.9 copy.130
  471.7 3.0 fusion.3
  476.2 9.7 %convolution_convert_fusion.1 = bf16[4096,512]{1,0:T(8,128)(2,1)} fusion(bf16[1024,4096]{1,0:T(8,128)(2,1)} %slice_dynamic-update-slice_fusion.16, bf16[1024,512]{0,1:T(8,128)(2,1)S(1)} %fusion.1), kind=kOutput, calls=%fused_computation.2 | convolution fusion | flops 4297064448 | bytes 13631488 | tf_op jit(solution)/shard_map/dot_general | solution.py:108
  487.1 10.6 %fusion.46 = f32[1024,4096]{1,0:T(8,128)} fusion(bf16[1024,512]{0,1:T(8,128)(2,1)S(1)} %copy-done.13, bf16[4096,512]{1,0:T(8,128)(2,1)} %all-gather.11.cloned.1.call-done), kind=kOutput, calls=%fused_computation.128 | convolution fusion | flops 4294967296 | bytes 22020096 | tf_op jit(solution)/shard_map/dot_general | solution.py:122
  497.7 8.1 %fusion.45 = f32[1024,4096]{1,0:T(8,128)} fusion(bf16[1024,512]{0,1:T(8,128)(2,1)S(1)} %copy-done.11, bf16[4096,512]{1,0:T(8,128)(2,1)S(1)} %copy-done.22), kind=kOutput, calls=%fused_computation.127 | convolution fusion | flops 4294967296 | bytes 22020096 | tf_op jit(solution)/shard_map/dot_general | solution.py:121
  505.8 19.2 %add_convert_fusion = bf16[1024,4096]{1,0:T(8,128)(2,1)} fusion(f32[1024,4096]{1,0:T(8,128)} %fusion.45, f32[1024,4096]{1,0:T(8,128)} %fusion.46, bf16[4096,512]{1,0:T(8,128)(2,1)} %all-gather.7.cloned.1.call-done, bf16[128,8,4,128]{3,2,1,0:T(4,128)(2,1)S(1)} %bitcast.198), kind=kOutput, calls=%fused_computation | convolution fusion | flops 4307550208 | bytes 47185920 | tf_op jit(solution)/shard_map/dot_general | solution.py:123
  525.0 1.9 slice_dynamic-update-slice_fusion.15
  530.8 2.0 slice_dynamic-update-slice_fusion.12
  538.5 1.9 slice_dynamic-update-slice_fusion.8
  540.5 2.0 slice_dynamic-update-slice_fusion.7
  542.4 1.9 slice_dynamic-update-slice_fusion.6
  552.0 2.0 slice_dynamic-update-slice_fusion.1
  557.1 28.1 %all_to_all.182 = bf16[4,256,512]{2,1,0:T(8,128)(2,1)S(1)} all-to-all(bf16[4,256,512]{2,1,0:T(8,128)(2,1)S(1)} %bitcast.218), channel_id=1, replica_groups=mesh['fa'=4,'fb'=4,'head'=2] {'fa'}, dimensions={0} | all-to-all | bytes 2097152 | tf_op jit(solution)/shard_map/all_to_all | solution.py:63
  585.1 28.8 %all_to_all.183 = bf16[4,256,512]{2,1,0:T(8,128)(2,1)S(1)} all-to-all(bf16[4,256,512]{2,1,0:T(8,128)(2,1)} %bitcast.219), channel_id=1, replica_groups=mesh['fa'=4,'fb'=4,'head'=2] {'fa'}, dimensions={0} | all-to-all | bytes 2097152 | tf_op jit(solution)/shard_map/all_to_all | solution.py:63
  613.9 6.2 all-to-all-start.13
  621.1 20.5 %all-to-all-done.13 = bf16[4,256,512]{2,1,0:T(8,128)(2,1)S(1)} async-done(((bf16[4,256,512]{2,1,0:T(8,128)(2,1)}), bf16[4,256,512]{2,1,0:T(8,128)(2,1)S(1)}, u32[]{:S(2)}, u32[]{:S(2)}) %all-to-all-start.13) | async-done | bytes 1048608 | tf_op jit(solution)/shard_map/all_to_all | solution.py:63
  646.4 9.1 %reduce-scatter.12.cloned.1.call-done = bf16[1024,2048]{1,0:T(8,128)(2,1)} async-done(((bf16[1024,4096]{1,0:T(8,128)(2,1)}), bf16[1024,2048]{1,0:T(8,128)(2,1)}) %reduce-scatter.12.cloned.1.call-update) | async-done | bytes 4194320 | tf_op jit(solution)/shard_map/reduce_scatter | solution.py:128
  655.5 80.2 %reduce-scatter.14.cloned.1.call-done = bf16[256,2048]{1,0:T(8,128)(2,1)} async-done(((bf16[1024,2048]{1,0:T(8,128)(2,1)}), bf16[256,2048]{1,0:T(8,128)(2,1)}) %reduce-scatter.14.cloned.1.call-update) | async-done | bytes 1048592 | tf_op jit(solution)/shard_map/reduce_scatter | solution.py:131
  (140 shorter events, 83.1 us)
Async XLA Ops:
  7.2 188.9 %all-gather.5.cloned.1.call-start = ((), (), s32[]{:S(2)}) async-start(), calls=%async_computation.19 | async-start | bytes 10485760 | tf_op jit(solution)/shard_map/all_gather | solution.py:65
  7.9 8.1 %copy-start.14 = (bf16[256,2048]{1,0:T(8,128)(2,1)S(1)}, bf16[256,2048]{1,0:T(8,128)(2,1)}, u32[]{:S(2)}) copy-start(bf16[256,2048]{1,0:T(8,128)(2,1)} %param.8) | copy-start | bytes 3145732
  10.7 62.4 %copy-start.15 = (bf16[256,2048]{1,0:T(8,128)(2,1)S(1)}, bf16[256,2048]{1,0:T(8,128)(2,1)}, u32[]{:S(2)}) copy-start(bf16[256,2048]{1,0:T(8,128)(2,1)} %param.9) | copy-start | bytes 3145732
  10.7 55.6 %all-to-all-start = ((bf16[4,256,512]{1,2,0:T(8,128)(2,1)}), bf16[4,256,512]{1,2,0:T(8,128)(2,1)S(1)}, u32[]{:S(2)}, u32[]{:S(2)}) async-start(bf16[4,256,512]{1,2,0:T(8,128)(2,1)} %copy.104), calls=%async_computation | async-start | bytes 2097152 | tf_op jit(solution)/shard_map/all_to_all | solution.py:63
  66.2 52.1 %all-to-all-start.1 = ((bf16[4,256,512]{2,1,0:T(8,128)(2,1)}), bf16[4,256,512]{2,1,0:T(8,128)(2,1)S(1)}, u32[]{:S(2)}, u32[]{:S(2)}) async-start(bf16[4,256,512]{2,1,0:T(8,128)(2,1)} %bitcast.4), calls=%async_computation.1 | async-start | bytes 2097152 | tf_op jit(solution)/shard_map/all_to_all | solution.py:63
  73.0 202.1 %all-gather.9.cloned.1.call-start = ((), (), s32[]{:S(2)}) async-start(), calls=%async_computation.21 | async-start | bytes 5242880 | tf_op jit(solution)/shard_map/all_gather | solution.py:71
  118.3 77.8 %copy-start.5 = (bf16[4,256,512]{2,1,0:T(8,128)(2,1)}, bf16[4,256,512]{2,1,0:T(8,128)(2,1)S(1)}, u32[]{:S(2)}) copy-start(bf16[4,256,512]{2,1,0:T(8,128)(2,1)S(1)} %all-to-all-done.1) | copy-start | bytes 3145732
  196.1 103.2 %all-gather.11.cloned.1.call-start = ((), (), s32[]{:S(2)}) async-start(), calls=%async_computation.22 | async-start | bytes 5242880 | tf_op jit(solution)/shard_map/all_gather | solution.py:71
  227.5 28.3 %all-to-all-start.3 = ((bf16[4,256,512]{2,1,0:T(8,128)(2,1)}), bf16[4,256,512]{2,1,0:T(8,128)(2,1)S(1)}, u32[]{:S(2)}, u32[]{:S(2)}) async-start(bf16[4,256,512]{2,1,0:T(8,128)(2,1)} %bitcast.211), calls=%async_computation.3 | async-start | bytes 2097152 | tf_op jit(solution)/shard_map/all_to_all | solution.py:63
  255.8 3.6 copy-start.4
  255.8 38.9 %all-to-all-start.2 = ((bf16[8,128,4,128]{3,0,2,1:T(8,128)(2,1)}), bf16[8,128,4,128]{3,0,2,1:T(8,128)(2,1)S(1)}, u32[]{:S(2)}, u32[]{:S(2)}) async-start(bf16[8,128,4,128]{3,0,2,1:T(8,128)(2,1)} %copy.107), calls=%async_computation.2 | async-start | bytes 2097152 | tf_op jit(solution)/shard_map/all_to_all | solution.py:81
  259.3 67.7 %all-gather.7.cloned.1.call-start = ((), (), s32[]{:S(2)}) async-start(), calls=%async_computation.20 | async-start | bytes 5242880 | tf_op jit(solution)/shard_map/all_gather | solution.py:71
  283.5 7.9 %copy-start = (f32[1024,512]{0,1:T(8,128)}, f32[1024,512]{0,1:T(8,128)S(1)}, u32[]{:S(2)}) copy-start(f32[1024,512]{0,1:T(8,128)S(1)} %get-tuple-element.65) | copy-start | bytes 6291460
  284.8 6.6 copy-start.20
  294.7 28.0 %all-to-all-start.5 = ((bf16[8,128,4,128]{3,2,0,1:T(4,128)(2,1)}), bf16[8,128,4,128]{3,2,0,1:T(4,128)(2,1)}, u32[]{:S(2)}, u32[]{:S(2)}) async-start(bf16[8,128,4,128]{3,2,0,1:T(4,128)(2,1)} %multiply_convert_fusion.1), calls=%async_computation.5 | async-start | bytes 2097152 | tf_op jit(solution)/shard_map/all_to_all | solution.py:81
  308.7 6.3 copy-start.21
  322.7 19.0 %all-to-all-start.7 = ((bf16[8,128,4,128]{3,2,0,1:T(4,128)(2,1)}), bf16[8,128,4,128]{3,2,0,1:T(4,128)(2,1)}, u32[]{:S(2)}, u32[]{:S(2)}) async-start(bf16[8,128,4,128]{3,2,0,1:T(4,128)(2,1)} %multiply_convert_fusion), calls=%async_computation.7 | async-start | bytes 2097152 | tf_op jit(solution)/shard_map/all_to_all | solution.py:81
  341.8 19.3 %all-to-all-start.4 = ((bf16[8,128,4,128]{3,2,0,1:T(4,128)(2,1)}), bf16[8,128,4,128]{3,2,0,1:T(4,128)(2,1)}, u32[]{:S(2)}, u32[]{:S(2)}) async-start(bf16[8,128,4,128]{3,2,0,1:T(4,128)(2,1)} %copy.110), calls=%async_computation.4 | async-start | bytes 2097152 | tf_op jit(solution)/shard_map/all_to_all | solution.py:81
  348.2 2.0 copy-start.6
  350.2 4.0 copy-start.7
  361.0 2.8 copy-start.1
  361.0 2.8 copy-start.8
  363.8 1.3 copy-start.9
  366.6 18.8 %all-to-all-start.8 = ((bf16[32,32,4,128]{3,2,1,0:T(4,128)(2,1)}), bf16[32,32,4,128]{3,2,1,0:T(4,128)(2,1)}, u32[]{:S(2)}, u32[]{:S(2)}) async-start(bf16[32,32,4,128]{3,2,1,0:T(4,128)(2,1)} %copy.121), calls=%async_computation.8 | async-start | bytes 2097152 | tf_op jit(solution)/shard_map/all_to_all | solution.py:84
  370.9 184.9 %reduce-scatter.6.cloned.1.call-start = ((), (), s32[]{:S(2)}) async-start(), calls=%async_computation.23 | async-start | bytes 5242880 | tf_op jit(solution)/shard_map/reduce_scatter | solution.py:111
  387.1 2.1 copy-start.3
  396.9 1.0 copy-start.10
  407.7 148.1 %reduce-scatter.10.cloned.1.call-start = ((), (), s32[]{:S(2)}) async-start(), calls=%async_computation.25 | async-start | bytes 5242880 | tf_op jit(solution)/shard_map/reduce_scatter | solution.py:111
  442.7 19.6 %all-to-all-start.9 = ((bf16[32,32,4,128]{3,2,1,0:T(4,128)(2,1)}), bf16[32,32,4,128]{3,2,1,0:T(4,128)(2,1)}, u32[]{:S(2)}, u32[]{:S(2)}) async-start(bf16[32,32,4,128]{3,2,1,0:T(4,128)(2,1)} %copy.127), calls=%async_computation.9 | async-start | bytes 2097152 | tf_op jit(solution)/shard_map/all_to_all | solution.py:84
  446.9 108.9 %reduce-scatter.8.cloned.1.call-start = ((), (), s32[]{:S(2)}) async-start(), calls=%async_computation.24 | async-start | bytes 5242880 | tf_op jit(solution)/shard_map/reduce_scatter | solution.py:111
  471.7 3.0 copy-start.2
  475.2 1.0 copy-start.12
  485.9 1.2 copy-start.13
  485.9 11.8 %copy-start.11 = (bf16[1024,512]{0,1:T(8,128)(2,1)S(1)}, bf16[1024,512]{0,1:T(8,128)(2,1)}, u32[]{:S(2)}) copy-start(bf16[1024,512]{0,1:T(8,128)(2,1)} %copy-done.10) | copy-start | bytes 3145732
  485.9 169.6 %reduce-scatter.12.cloned.1.call-start = ((), (), s32[]{:S(2)}) async-start(), calls=%async_computation.26 | async-start | bytes 12582912 | tf_op jit(solution)/shard_map/reduce_scatter | solution.py:128
  487.1 10.6 %copy-start.22 = (bf16[4096,512]{1,0:T(8,128)(2,1)S(1)}, bf16[4096,512]{1,0:T(8,128)(2,1)}, u32[]{:S(2)}) copy-start(bf16[4096,512]{1,0:T(8,128)(2,1)} %all-gather.9.cloned.1.call-done) | copy-start | bytes 12582916
  555.8 1.2 copy-start.16
  613.9 27.7 %all-to-all-start.13 = ((bf16[4,256,512]{2,1,0:T(8,128)(2,1)}), bf16[4,256,512]{2,1,0:T(8,128)(2,1)S(1)}, u32[]{:S(2)}, u32[]{:S(2)}) async-start(bf16[4,256,512]{2,1,0:T(8,128)(2,1)} %bitcast.217), calls=%async_computation.17 | async-start | bytes 2097152 | tf_op jit(solution)/shard_map/all_to_all | solution.py:63
  620.1 115.6 %reduce-scatter.14.cloned.1.call-start = ((), (), s32[]{:S(2)}) async-start(), calls=%async_computation.27 | async-start | bytes 5242880 | tf_op jit(solution)/shard_map/reduce_scatter | solution.py:131
  621.1 23.7 %copy-start.17 = (bf16[256,512]{1,0:T(8,128)(2,1)S(1)}, bf16[256,512]{1,0:T(8,128)(2,1)}, u32[]{:S(2)}) copy-start(bf16[256,512]{1,0:T(8,128)(2,1)} %get-tuple-element.39) | copy-start | bytes 786436
  621.1 23.7 %copy-start.18 = (bf16[256,512]{1,0:T(8,128)(2,1)S(1)}, bf16[256,512]{1,0:T(8,128)(2,1)}, u32[]{:S(2)}) copy-start(bf16[256,512]{1,0:T(8,128)(2,1)} %get-tuple-element.40) | copy-start | bytes 786436
  621.1 23.7 %copy-start.19 = (bf16[256,512]{1,0:T(8,128)(2,1)S(1)}, bf16[256,512]{1,0:T(8,128)(2,1)}, u32[]{:S(2)}) copy-start(bf16[256,512]{1,0:T(8,128)(2,1)} %get-tuple-element.41) | copy-start | bytes 786436
Sparse Core Ops, SparseCore 0:
  9.5 186.4 all-gather.4
  198.2 36.6 all-gather.8
  236.4 41.2 all-gather.10
  279.2 42.8 all-gather.6
  407.8 45.4 reduce-scatter.5
  455.7 44.8 reduce-scatter.9
  503.1 44.5 reduce-scatter.7
  556.0 99.4 reduce-scatter.11
  658.4 77.2 reduce-scatter.13
where the time goes:
time: 754 us; the launch traced here: 743 us
  waiting for transfers between devices  320 us (42%)
  local copies, waits for them, and re-layouts  123 us (16%)
  matrix products  107 us (14%)
  blocking collectives  105 us (14%)
  starting transfers between devices  50.9 us (7%)
  other arithmetic  21.2 us (3%)
  between operations  14.8 us (2%)
    all_to_all x4, waiting for transfers between devices, exchange(): return lax.all_to_all(x, 'fa', split_axis=0, concat_axis=0, tiled=True)  116 us
    all_to_all x3, blocking collectives, exchange(): return lax.all_to_all(x, 'fa', split_axis=0, concat_axis=0, tiled=True)  88.2 us
    reduce_scatter x1, waiting for transfers between devices, body(): lax.psum_scatter(partial, 'fa', scatter_dimension=0, tiled=True)  80.2 us
    all_gather x1, waiting for transfers between devices, body(): lax.all_gather(activations.reshape(-1, width), 'fa', axis=0, tiled=True)  77.7 us
    unnamed x82, local copies, waits for them, and re-layouts  68.5 us
    dot_general x3, matrix products, weight_grad(): lax.dot_general(rows, d, (((0,), (0,)), ((), ())), preferred_element_type...  29.3 us
    all_to_all x2, waiting for transfers between devices, back(): return lax.all_to_all(x, 'fb', split_axis=0, concat_axis=1, tiled=True)  24.8 us
    all_to_all x4, starting transfers between devices, exchange(): return lax.all_to_all(x, 'fa', split_axis=0, concat_axis=0, tiled=True)  24.6 us
  transfers between devices with their start and end apart: 19, of which 11 were waited for; matrix products, arithmetic and copies ran while one was open for 30% of the time, Pallas kernels for 0%

commit v1 on v0

--- a/solution.py
+++ b/solution.py
@@ -135,10 +135,124 @@
     return body
 
 
+def make_patch_body(n_frame):
+    swap = [(0, 1), (1, 0)]
+
+    def body(activations, w_query, w_key, w_value, q_gain, k_gain, grad_attn):
+        frames_here, patches, width = activations.shape
+        rows_here, head_cols = w_query.shape
+        half = patches // 2
+        cols = head_cols // n_frame
+        frames = frames_here * n_frame
+        tokens = frames * half
+        side = lax.axis_index("head")
+
+        def halves(x, axis, size):
+            mine = lax.dynamic_slice_in_dim(x, side * size, size, axis)
+            other = lax.dynamic_slice_in_dim(x, (1 - side) * size, size, axis)
+            return mine, other
+
+        def rejoin(mine, other, axis):
+            return jnp.where(
+                side == 0,
+                jnp.concatenate([mine, other], axis),
+                jnp.concatenate([other, mine], axis),
+            )
+
+        def exchange(x):
+            return lax.all_to_all(x, "frame", split_axis=0, concat_axis=0, tiled=True)
+
+        def across(x):
+            return lax.ppermute(x, "head", swap)
+
+        def by_head(x):
+            return jnp.concatenate([x[:, i * cols : (i + 1) * cols] for i in range(n_frame)], axis=0)
+
+        own_acts, _ = halves(activations, 1, half)
+        acts = lax.all_gather(own_acts.reshape(-1, width), "frame", axis=0, tiled=True)
+
+        cot_mine, cot_other = halves(grad_attn, 1, half)
+        cot_other = across(cot_other)
+        mine = [exchange(by_head(w)) for w in (w_query, w_key, w_value)]
+        wq, wk, wv = (jnp.concatenate([w, across(w)], axis=1) for w in mine)
+        cotan = jnp.concatenate(
+            [
+                exchange(by_head(x.reshape(-1, head_cols)))
+                for x in (cot_mine, cot_other)
+            ],
+            axis=1,
+        )
+
+        heads = 2 * cols // HD
+        shape4 = (frames, half, heads, HD)
+        shape3 = (tokens, heads, HD)
+        q_raw = jnp.dot(acts, wq, preferred_element_type=jnp.float32).reshape(shape3)
+        k_raw = jnp.dot(acts, wk, preferred_element_type=jnp.float32).reshape(shape3)
+        value = jnp.dot(acts, wv, preferred_element_type=jnp.float32)
+        value = value.astype(jnp.bfloat16).reshape(shape4)
+        q_norm = scaled(q_raw, q_gain).astype(jnp.bfloat16).reshape(shape4)
+        k_norm = scaled(k_raw, k_gain).astype(jnp.bfloat16).reshape(shape4)
+        d_qn, d_kn, d_val = attend_back(q_norm, k_norm, value, cotan.reshape(shape4))
+
+        _, pull_query = jax.vjp(lambda raw: scaled(raw, q_gain), q_raw)
+        _, pull_key = jax.vjp(lambda raw: scaled(raw, k_gain), k_raw)
+        d_q = pull_query(d_qn.reshape(shape3).astype(jnp.float32))[0]
+        d_q = d_q.astype(jnp.bfloat16).reshape(tokens, 2 * cols)
+        d_k = pull_key(d_kn.reshape(shape3).astype(jnp.float32))[0]
+        d_k = d_k.astype(jnp.bfloat16).reshape(tokens, 2 * cols)
+        d_v = d_val.reshape(tokens, 2 * cols)
+
+        d_all = jnp.concatenate([d_q, d_k, d_v], axis=1)
+        w_all = jnp.concatenate([wq, wk, wv], axis=1)
+        partial = lax.dot_general(
+            d_all, w_all, (((1,), (1,)), ((), ())), preferred_element_type=jnp.float32
+        ).astype(jnp.bfloat16)
+        partial = lax.psum_scatter(partial, "frame", scatter_dimension=0, tiled=True)
+        mine_cols, other_cols = halves(partial, 1, head_cols)
+        shape_out = (frames_here, half, head_cols)
+        grad_input = rejoin(
+            mine_cols.reshape(shape_out), across(other_cols).reshape(shape_out), 1
+        )
+
+        def weight_grad(d):
+            term = lax.dot_general(
+                acts, d, (((0,), (0,)), ((), ())), preferred_element_type=jnp.float32
+            )
+            total = term[:, :cols] + across(term[:, cols:].astype(jnp.bfloat16)).astype(jnp.float32)
+            out = exchange(total.astype(jnp.bfloat16))
+            out = [out[i * rows_here : (i + 1) * rows_here] for i in range(n_frame)]
+            return jnp.concatenate(out, axis=1).astype(jnp.float32)
+
+        return (grad_input, weight_grad(d_q), weight_grad(d_k), weight_grad(d_v))
+
+    return body
+
+
 def solution(mesh):
     n_frame, n_head = mesh.shape["frame"], mesh.shape["head"]
 
+    def by_patch(activations, w_query, w_key, w_value, q_gain, k_gain, grad_attn):
+        placed = (
+            P("frame", None, None),
+            P("frame", "head"),
+            P("frame", "head"),
+            P("frame", "head"),
+            P(),
+            P(),
+            P("frame", None, "head"),
+        )
+        return jax.shard_map(
+            make_patch_body(n_frame),
+            mesh=mesh,
+            in_specs=placed,
+            out_specs=(placed[6], placed[1], placed[1], placed[1]),
+            check_vma=False,
+        )(activations, w_query, w_key, w_value, q_gain, k_gain, grad_attn)
+
     def run(activations, w_query, w_key, w_value, q_gain, k_gain, grad_attn):
+        heads_here = w_query.shape[1] // (HD * n_head)
+        if n_head == 2 and heads_here % n_frame == 0 and activations.shape[1] % n_head == 0:
+            return by_patch(activations, w_query, w_key, w_value, q_gain, k_gain, grad_attn)
         n_a = line_split(n_frame, w_query.shape[1] // (HD * n_head))
         n_b = n_frame // n_a
         split = Mesh(mesh.devices.reshape(n_a, n_b, n_head), ("fa", "fb", "head"))

time: 754 us -> 673 us (0.89)
  blocking collectives: 105 us -> 0 us
  local copies, waits for them, and re-layouts: 123 us -> 165 us
  waiting for transfers between devices: 320 us -> 304 us
  matrix products: 107 us -> 91.8 us
  other arithmetic: 21.2 us -> 30.1 us
    all_to_all x4 -> x0, blocking collectives: 105 us -> none  [the longest x3 88.2 us: exchange(): return lax.all_to_all(x, 'fa', split_axis=0, concat_axis=0, tiled=True)]
    all_gather x4 -> x1, waiting for transfers between devices: 77.8 us -> 0.01 us  [body(): lax.all_gather(own_acts.reshape(-1, width), 'frame', axis=0, tiled=True)]
    ppermute x0 -> x8, waiting for transfers between devices: none -> 70.5 us  [across(): return lax.ppermute(x, 'head', swap)]
    reduce_scatter x5 -> x1, waiting for transfers between devices: 89.3 us -> 47.3 us  [body(): lax.psum_scatter(partial, 'frame', scatter_dimension=0, tiled=True)]
    all_to_all x10 -> x8, waiting for transfers between devices: 152 us -> 186 us  [exchange(): return lax.all_to_all(x, 'frame', split_axis=0, concat_axis=0, tiled=True)]
    unnamed x82 -> x168, local copies, waits for them, and re-layouts: 68.5 us -> 97.8 us
    convert_element_type x8 -> x6, local copies, waits for them, and re-layouts: 14.1 us -> 28.1 us  [the longest x3 14.8 us: body(): d_k = pull_key(d_kn.reshape(shape3).astype(jnp.float32))[0]]
    dot_general x9 -> x7, matrix products: 93.9 us -> 81.7 us  [the longest x3 30.3 us: weight_grad(): lax.dot_general(acts, d, (((0,), (0,)), ((), ())), preferred_element_type...]
  transfers between devices with their start and end apart: 19 -> 18, of which waited for: 11 -> 13; matrix products, arithmetic and copies ran while one was open for 30% -> 22% of each run, Pallas kernels for 0% -> 0%
where the time goes in v1:
time: 673 us; the launch traced here: 660 us
  waiting for transfers between devices  304 us (45%)
  local copies, waits for them, and re-layouts  165 us (25%)
  matrix products  91.8 us (14%)
  starting transfers between devices  54.3 us (8%)
  other arithmetic  30.1 us (4%)
  between operations  15 us (2%)
    all_to_all x8, waiting for transfers between devices, exchange(): return lax.all_to_all(x, 'frame', split_axis=0, concat_axis=0, tiled=True)  186 us
    unnamed x168, local copies, waits for them, and re-layouts  97.8 us
    ppermute x8, waiting for transfers between devices, across(): return lax.ppermute(x, 'head', swap)  70.5 us
    reduce_scatter x1, waiting for transfers between devices, body(): lax.psum_scatter(partial, 'frame', scatter_dimension=0, tiled=True)  47.3 us
    all_to_all x8, starting transfers between devices, exchange(): return lax.all_to_all(x, 'frame', split_axis=0, concat_axis=0, tiled=True)  43.2 us
    dot_general x3, matrix products, weight_grad(): lax.dot_general(acts, d, (((0,), (0,)), ((), ())), preferred_element_type...  30.3 us
    dot_general x1, matrix products, body(): lax.dot_general(d_all, w_all, (((1,), (1,)), ((), ())), preferred_element...  19.1 us
    convert_element_type x3, local copies, waits for them, and re-layouts, body(): d_k = pull_key(d_kn.reshape(shape3).astype(jnp.float32))[0]  14.8 us
  transfers between devices with their start and end apart: 18, of which 13 were waited for; matrix products, arithmetic and copies ran while one was open for 22% of the time, Pallas kernels for 0%

profile of v1, /device:TPU:16, one launch (start us, length us, event | category | flops | bytes accessed | tf_op | source)
XLA Modules:
  0.0 659.9 jit_solution(15058171025865757138)
XLA Ops:
  7.2 1.5 copy-done
  20.7 6.2 all-to-all-start
  56.5 6.0 all-to-all-start.1
  66.8 12.8 %all-to-all-done.1 = bf16[16,128,128]{2,1,0:T(8,128)(2,1)S(1)} async-done(((bf16[16,128,128]{2,1,0:T(8,128)(2,1)}), bf16[16,128,128]{2,1,0:T(8,128)(2,1)S(1)}, u32[]{:S(2)}, u32[]{:S(2)}) %all-to-all-start.1) | async-done | bytes 524320 | tf_op jit(solution)/shard_map/all_to_all | solution.py:163
  79.5 5.0 all-to-all-start.3
  86.3 1.5 constant_dynamic-update-slice_fusion.47
  96.7 41.9 %all-to-all-done.3 = bf16[16,256,128]{2,1,0:T(8,128)(2,1)S(1)} async-done(((bf16[16,256,128]{2,1,0:T(8,128)(2,1)}), bf16[16,256,128]{2,1,0:T(8,128)(2,1)S(1)}, u32[]{:S(2)}, u32[]{:S(2)}) %all-to-all-start.3) | async-done | bytes 1048608 | tf_op jit(solution)/shard_map/all_to_all | solution.py:163
  138.6 4.8 all-to-all-start.4
  156.7 34.7 %all-to-all-done.4 = bf16[16,256,128]{2,1,0:T(8,128)(2,1)S(1)} async-done(((bf16[16,256,128]{2,1,0:T(8,128)(2,1)}), bf16[16,256,128]{2,1,0:T(8,128)(2,1)S(1)}, u32[]{:S(2)}, u32[]{:S(2)}) %all-to-all-start.4) | async-done | bytes 1048608 | tf_op jit(solution)/shard_map/all_to_all | solution.py:163
  191.4 4.7 all-to-all-start.2
  196.1 1.6 collective-permute-start.2
  201.8 19.5 %all-to-all-done.2 = bf16[16,256,128]{2,1,0:T(8,128)(2,1)} async-done(((bf16[16,256,128]{2,1,0:T(8,128)(2,1)}), bf16[16,256,128]{2,1,0:T(8,128)(2,1)}, u32[]{:S(2)}, u32[]{:S(2)}) %all-to-all-start.2) | async-done | bytes 1048608 | tf_op jit(solution)/shard_map/all_to_all | solution.py:163
  222.8 2.3 constant_dynamic-update-slice_fusion.84
  226.3 18.5 %collective-permute-done.3 = bf16[4096,128]{1,0:T(8,128)(2,1)} collective-permute-done((bf16[4096,128]{1,0:T(8,128)(2,1)S(1)}, bf16[4096,128]{1,0:T(8,128)(2,1)}, u32[]{:S(2)}, u32[]{:S(2)}) %collective-permute-start.3) | collective-permute-done | bytes 1048608 | tf_op jit(solution)/shard_map/ppermute | solution.py:166
  244.8 2.3 constant_dynamic-update-slice_fusion.82
  247.1 2.4 constant_dynamic-update-slice_fusion.81
  249.5 16.8 %collective-permute-done.1 = bf16[4096,128]{1,0:T(8,128)(2,1)S(1)} collective-permute-done((bf16[4096,128]{1,0:T(8,128)(2,1)}, bf16[4096,128]{1,0:T(8,128)(2,1)S(1)}, u32[]{:S(2)}, u32[]{:S(2)}) %collective-permute-start.1) | collective-permute-done | bytes 1048608 | tf_op jit(solution)/shard_map/ppermute | solution.py:166
  268.4 11.0 %convolution_convert_fusion.1 = bf16[2048,256]{1,0:T(8,128)(2,1)S(1)} fusion(bf16[2048,4096]{1,0:T(8,128)(2,1)} %all-gather.2.cloned.1.call-done, bf16[4096,128]{1,0:T(8,128)(2,1)} %copy-done.14, bf16[4096,128]{1,0:T(8,128)(2,1)} %bitcast.9), kind=kOutput, calls=%fused_computation.8 | convolution fusion | flops 4299685888 | bytes 19922944 | tf_op jit(solution)/shard_map/dot_general | solution.py:191
  280.5 9.0 %multiply_reduce_fusion.2 = (f32[2048,2]{0,1:T(2,128)S(1)}, f32[2048,256]{0,1:T(8,128)S(1)}) fusion(bf16[2048,4096]{1,0:T(8,128)(2,1)} %all-gather.2.cloned.1.call-done, bf16[4096,128]{1,0:T(8,128)(2,1)} %collective-permute-done.2, bf16[4096,128]{1,0:T(8,128)(2,1)} %bitcast.295), kind=kOutput, calls=%fused_computation.51 | convolution fusion | flops 4300206080 | bytes 20987904 | tf_op jit(solution)/shard_map/dot_general | solution.py:189
  289.7 12.2 %multiply_reduce_fusion.1 = (f32[2048,2]{0,1:T(2,128)S(1)}, f32[2048,256]{0,1:T(8,128)}) fusion(bf16[2048,4096]{1,0:T(8,128)(2,1)} %all-gather.2.cloned.1.call-done, bf16[4096,128]{1,0:T(8,128)(2,1)} %collective-permute-done.3, bf16[4096,128]{1,0:T(8,128)(2,1)} %bitcast.298), kind=kOutput, calls=%fused_computation.49 | convolution fusion | flops 4300206080 | bytes 20987904 | tf_op jit(solution)/shard_map/dot_general | solution.py:190
  302.0 4.9 reshape.208
  306.9 4.6 copy.46
  311.5 3.0 reshape.207
  314.5 4.6 copy.43
  319.0 3.2 multiply_convert_fusion
  322.3 2.2 fusion.51
  324.5 1.8 fusion.30
  326.3 1.8 multiply_reduce_fusion
  328.2 2.9 convert_bitcast_fusion
  333.8 2.6 copy.53
  336.4 5.7 copy.67
  342.1 4.1 copy.58
  346.2 5.8 copy.68
  351.9 1.8 copy.54
  353.8 2.9 copy.59
  356.7 2.3 copy.60
  360.1 2.3 copy.61
  362.4 2.8 fusion.24
  365.2 5.0 reshape.209
  370.2 2.8 fusion.22
  373.1 5.0 reshape.210
  378.1 3.3 fusion.5
  381.4 1.6 fusion.6
  383.0 19.1 %convolution_convert_fusion = bf16[2048,4096]{1,0:T(8,128)(2,1)} fusion(bf16[4096,768]{1,0:T(8,128)(2,1)} %constant_dynamic-update-slice_fusion.80, bf16[2048,256]{0,1:T(8,128)(2,1)S(1)} %copy-done.13, bf16[2048,256]{0,1:T(8,128)(2,1)} %fusion.6, bf16[2048,256]{0,1:T(8,128)(2,1)S(1)} %copy-done.16), kind=kOutput, calls=%fused_computation | convolution fusion | flops 12902727680 | bytes 26214400 | tf_op jit(solution)/shard_map/dot_general | solution.py:207
  402.1 8.7 %fusion.50 = f32[4096,256]{1,0:T(8,128)S(1)} fusion(bf16[2048,4096]{1,0:T(8,128)(2,1)} %all-gather.2.cloned.1.call-done, bf16[256,8,2,128]{3,2,1,0:T(2,128)(2,1)S(1)} %bitcast.300), kind=kOutput, calls=%fused_computation.270 | convolution fusion | flops 4294967296 | bytes 22020096 | tf_op jit(solution)/shard_map/dot_general | solution.py:218
  411.0 1.6 collective-permute-start.7
  412.5 11.6 %fusion.53 = f32[4096,256]{1,0:T(8,128)S(1)} fusion(bf16[2048,4096]{1,0:T(8,128)(2,1)} %all-gather.2.cloned.1.call-done, bf16[2048,256]{0,1:T(8,128)(2,1)S(1)} %copy-done.18), kind=kOutput, calls=%fused_computation.273 | convolution fusion | flops 4294967296 | bytes 22020096 | tf_op jit(solution)/shard_map/dot_general | solution.py:218
  426.4 10.0 %fusion.52 = f32[4096,256]{1,0:T(8,128)S(1)} fusion(bf16[2048,4096]{1,0:T(8,128)(2,1)} %all-gather.2.cloned.1.call-done, bf16[2048,256]{0,1:T(8,128)(2,1)S(1)} %copy-done.17), kind=kOutput, calls=%fused_computation.272 | convolution fusion | flops 4294967296 | bytes 22020096 | tf_op jit(solution)/shard_map/dot_general | solution.py:218
  439.2 6.0 all-to-all-start.7
  445.3 14.4 %collective-permute-done.6 = bf16[4096,128]{1,0:T(8,128)(2,1)} collective-permute-done((bf16[4096,128]{1,0:T(8,128)(2,1)S(1)}, bf16[4096,128]{1,0:T(8,128)(2,1)}, u32[]{:S(2)}, u32[]{:S(2)}) %collective-permute-start.6) | collective-permute-done | bytes 1048608 | tf_op jit(solution)/shard_map/ppermute | solution.py:166
  459.6 3.0 fusion.8
  462.7 17.7 %collective-permute-done.5 = bf16[4096,128]{1,0:T(8,128)(2,1)} collective-permute-done((bf16[4096,128]{1,0:T(8,128)(2,1)S(1)}, bf16[4096,128]{1,0:T(8,128)(2,1)}, u32[]{:S(2)}, u32[]{:S(2)}) %collective-permute-start.5) | collective-permute-done | bytes 1048608 | tf_op jit(solution)/shard_map/ppermute | solution.py:166
  480.4 2.5 fusion.9
  482.9 13.4 %all-to-all-done.7 = bf16[16,256,128]{2,1,0:T(8,128)(2,1)S(1)} async-done(((bf16[16,256,128]{2,1,0:T(8,128)(2,1)}), bf16[16,256,128]{2,1,0:T(8,128)(2,1)S(1)}, u32[]{:S(2)}, u32[]{:S(2)}) %all-to-all-start.7) | async-done | bytes 1048608 | tf_op jit(solution)/shard_map/all_to_all | solution.py:163
  496.3 5.2 all-to-all-start.6
  511.6 38.6 %all-to-all-done.6 = bf16[16,256,128]{2,1,0:T(8,128)(2,1)S(1)} async-done(((bf16[16,256,128]{2,1,0:T(8,128)(2,1)}), bf16[16,256,128]{2,1,0:T(8,128)(2,1)S(1)}, u32[]{:S(2)}, u32[]{:S(2)}) %all-to-all-start.6) | async-done | bytes 1048608 | tf_op jit(solution)/shard_map/all_to_all | solution.py:163
  550.2 5.4 all-to-all-start.5
  556.0 24.8 %all-to-all-done.5 = bf16[16,256,128]{2,1,0:T(8,128)(2,1)S(1)} async-done(((bf16[16,256,128]{2,1,0:T(8,128)(2,1)}), bf16[16,256,128]{2,1,0:T(8,128)(2,1)S(1)}, u32[]{:S(2)}, u32[]{:S(2)}) %all-to-all-start.5) | async-done | bytes 1048608 | tf_op jit(solution)/shard_map/all_to_all | solution.py:163
  589.1 47.3 %reduce-scatter.2.cloned.1.call-done = bf16[128,4096]{1,0:T(8,128)(2,1)} async-done(((bf16[2048,4096]{1,0:T(8,128)(2,1)}), bf16[128,4096]{1,0:T(8,128)(2,1)}) %reduce-scatter.2.cloned.1.call-update) | async-done | bytes 1048592 | tf_op jit(solution)/shard_map/reduce_scatter | solution.py:210
  637.7 1.5 collective-permute-start.4
  639.8 2.8 convert_element_type.130
  642.6 1.6 convert_element_type.127
  645.5 2.8 convert_element_type.124
  648.3 3.1 collective-permute-done.4
  (210 shorter events, 112.2 us)
Async XLA Ops:
  7.2 1.6 copy-start
  7.2 2.7 copy-start.15
  7.2 261.2 %all-gather.2.cloned.1.call-start = ((), (), s32[]{:S(2)}) async-start(), calls=%async_computation.9 | async-start | bytes 17825792 | tf_op jit(solution)/shard_map/all_gather | solution.py:172
  9.9 18.6 %copy-start.12 = (bf16[256,2048]{1,0:T(8,128)(2,1)S(1)}, bf16[256,2048]{1,0:T(8,128)(2,1)}, u32[]{:S(2)}) copy-start(bf16[256,2048]{1,0:T(8,128)(2,1)} %param.8) | copy-start | bytes 3145732
  20.7 35.7 %all-to-all-start = ((bf16[16,128,128]{2,1,0:T(8,128)(2,1)}), bf16[16,128,128]{2,1,0:T(8,128)(2,1)S(1)}, u32[]{:S(2)}, u32[]{:S(2)}) async-start(bf16[16,128,128]{2,1,0:T(8,128)(2,1)} %bitcast.1), calls=%async_computation | async-start | bytes 1048576 | tf_op jit(solution)/shard_map/all_to_all | solution.py:163
  26.9 19.6 %collective-permute-start = (bf16[2,64,2048]{2,1,0:T(8,128)(2,1)}, bf16[2,64,2048]{2,1,0:T(8,128)(2,1)S(1)}, u32[]{:S(2)}, u32[]{:S(2)}) collective-permute-start(bf16[2,64,2048]{2,1,0:T(8,128)(2,1)} %get-tuple-element.7), channel_id=1, source_target_pairs={{0,1},{1,0},{2,3},{3,2},{4,5},{5,4},{6,7},{7,6},{8,9},{9,8},{10,11... | collective-permute-start | bytes 1572872 | tf_op jit(solution)/shard_map/ppermute | solution.py:166
  56.5 23.0 %all-to-all-start.1 = ((bf16[16,128,128]{2,1,0:T(8,128)(2,1)}), bf16[16,128,128]{2,1,0:T(8,128)(2,1)S(1)}, u32[]{:S(2)}, u32[]{:S(2)}) async-start(bf16[16,128,128]{2,1,0:T(8,128)(2,1)} %bitcast.4), calls=%async_computation.1 | async-start | bytes 1048576 | tf_op jit(solution)/shard_map/all_to_all | solution.py:163
  79.5 59.1 %all-to-all-start.3 = ((bf16[16,256,128]{2,1,0:T(8,128)(2,1)}), bf16[16,256,128]{2,1,0:T(8,128)(2,1)S(1)}, u32[]{:S(2)}, u32[]{:S(2)}) async-start(bf16[16,256,128]{2,1,0:T(8,128)(2,1)} %bitcast.10), calls=%async_computation.3 | async-start | bytes 2097152 | tf_op jit(solution)/shard_map/all_to_all | solution.py:163
  86.3 52.3 %copy-start.11 = (bf16[4096,128]{1,0:T(8,128)(2,1)}, bf16[4096,128]{1,0:T(8,128)(2,1)S(1)}, u32[]{:S(2)}) copy-start(bf16[4096,128]{1,0:T(8,128)(2,1)S(1)} %constant_dynamic-update-slice_fusion.64) | copy-start | bytes 3145732
  138.6 62.1 %copy-start.6 = (bf16[16,256,128]{2,1,0:T(8,128)(2,1)}, bf16[16,256,128]{2,1,0:T(8,128)(2,1)S(1)}, u32[]{:S(2)}) copy-start(bf16[16,256,128]{2,1,0:T(8,128)(2,1)S(1)} %all-to-all-done.3) | copy-start | bytes 3145732
  138.6 52.8 %all-to-all-start.4 = ((bf16[16,256,128]{2,1,0:T(8,128)(2,1)}), bf16[16,256,128]{2,1,0:T(8,128)(2,1)S(1)}, u32[]{:S(2)}, u32[]{:S(2)}) async-start(bf16[16,256,128]{2,1,0:T(8,128)(2,1)} %bitcast.322), calls=%async_computation.4 | async-start | bytes 2097152 | tf_op jit(solution)/shard_map/all_to_all | solution.py:163
  143.4 54.3 %copy-start.19 = (f32[128]{0:T(128)S(1)}, f32[128]{0:T(128)}, u32[]{:S(2)}) copy-start(f32[128]{0:T(128)} %param.11) | copy-start | bytes 1540
  143.4 54.3 %copy-start.20 = (f32[128]{0:T(128)S(1)}, f32[128]{0:T(128)}, u32[]{:S(2)}) copy-start(f32[128]{0:T(128)} %param.12) | copy-start | bytes 1540
  191.4 33.8 %copy-start.7 = (bf16[16,256,128]{2,1,0:T(8,128)(2,1)}, bf16[16,256,128]{2,1,0:T(8,128)(2,1)S(1)}, u32[]{:S(2)}) copy-start(bf16[16,256,128]{2,1,0:T(8,128)(2,1)S(1)} %all-to-all-done.4) | copy-start | bytes 3145732
  191.4 29.9 %all-to-all-start.2 = ((bf16[16,256,128]{2,1,0:T(8,128)(2,1)}), bf16[16,256,128]{2,1,0:T(8,128)(2,1)}, u32[]{:S(2)}, u32[]{:S(2)}) async-start(bf16[16,256,128]{2,1,0:T(8,128)(2,1)} %bitcast.8), calls=%async_computation.2 | async-start | bytes 2097152 | tf_op jit(solution)/shard_map/all_to_all | solution.py:163
  196.1 440.3 %reduce-scatter.2.cloned.1.call-start = ((), (), s32[]{:S(2)}) async-start(), calls=%async_computation.10 | async-start | bytes 17825792 | tf_op jit(solution)/shard_map/reduce_scatter | solution.py:210
  196.1 26.7 %collective-permute-start.2 = (bf16[4096,128]{1,0:T(8,128)(2,1)S(1)}, bf16[4096,128]{1,0:T(8,128)(2,1)}, u32[]{:S(2)}, u32[]{:S(2)}) collective-permute-start(bf16[4096,128]{1,0:T(8,128)(2,1)S(1)} %bitcast.293), channel_id=1, source_target_pairs={{0,1},{1,0},{2,3},{3,2},{4,5},{5,4},{6,7},{7,6},{8,9},{9,8},{10,11... | collective-permute-start | bytes 3145736 | tf_op jit(solution)/shard_map/ppermute | solution.py:166
  200.1 44.7 %collective-permute-start.3 = (bf16[4096,128]{1,0:T(8,128)(2,1)S(1)}, bf16[4096,128]{1,0:T(8,128)(2,1)}, u32[]{:S(2)}, u32[]{:S(2)}) collective-permute-start(bf16[4096,128]{1,0:T(8,128)(2,1)S(1)} %bitcast.296), channel_id=1, source_target_pairs={{0,1},{1,0},{2,3},{3,2},{4,5},{5,4},{6,7},{7,6},{8,9},{9,8},{10,11... | collective-permute-start | bytes 3145736 | tf_op jit(solution)/shard_map/ppermute | solution.py:166
  221.3 45.0 %collective-permute-start.1 = (bf16[4096,128]{1,0:T(8,128)(2,1)}, bf16[4096,128]{1,0:T(8,128)(2,1)S(1)}, u32[]{:S(2)}, u32[]{:S(2)}) collective-permute-start(bf16[4096,128]{1,0:T(8,128)(2,1)} %bitcast.9), channel_id=1, source_target_pairs={{0,1},{1,0},{2,3},{3,2},{4,5},{5,4},{6,7},{7,6},{8,9},{9,8},{10,11... | collective-permute-start | bytes 3145736 | tf_op jit(solution)/shard_map/ppermute | solution.py:166
  266.3 1.0 copy-start.14
  324.5 1.8 copy-start.5
  332.5 1.3 copy-start.4
  378.1 3.3 copy-start.2
  378.1 3.3 copy-start.3
  381.4 1.6 copy-start.13
  381.4 1.6 copy-start.16
  410.8 1.7 copy-start.18
  411.0 27.1 %collective-permute-start.7 = (bf16[4096,128]{1,0:T(8,128)(2,1)S(1)}, bf16[4096,128]{1,0:T(8,128)(2,1)S(1)}, u32[]{:S(2)}, u32[]{:S(2)}) collective-permute-start(bf16[4096,128]{1,0:T(8,128)(2,1)S(1)} %slice.1053), channel_id=1, source_target_pairs={{0,1},{1,0},{2,3},{3,2},{4,5},{5,4},{6,7},{7,6},{8,9},{9,8},{10,11... | collective-permute-start | bytes 3145736 | tf_op jit(solution)/shard_map/ppermute | solution.py:166
  424.2 12.3 %copy-start.8 = (f32[4096,256]{1,0:T(8,128)}, f32[4096,256]{1,0:T(8,128)S(1)}, u32[]{:S(2)}) copy-start(f32[4096,256]{1,0:T(8,128)S(1)} %fusion.53) | copy-start | bytes 12582916
  424.2 2.2 copy-start.17
  424.3 35.3 %collective-permute-start.6 = (bf16[4096,128]{1,0:T(8,128)(2,1)S(1)}, bf16[4096,128]{1,0:T(8,128)(2,1)}, u32[]{:S(2)}, u32[]{:S(2)}) collective-permute-start(bf16[4096,128]{1,0:T(8,128)(2,1)S(1)} %slice.1054), channel_id=1, source_target_pairs={{0,1},{1,0},{2,3},{3,2},{4,5},{5,4},{6,7},{7,6},{8,9},{9,8},{10,11... | collective-permute-start | bytes 3145736 | tf_op jit(solution)/shard_map/ppermute | solution.py:166
  436.5 2.7 copy-start.9
  436.6 43.8 %collective-permute-start.5 = (bf16[4096,128]{1,0:T(8,128)(2,1)S(1)}, bf16[4096,128]{1,0:T(8,128)(2,1)}, u32[]{:S(2)}, u32[]{:S(2)}) collective-permute-start(bf16[4096,128]{1,0:T(8,128)(2,1)S(1)} %slice.1055), channel_id=1, source_target_pairs={{0,1},{1,0},{2,3},{3,2},{4,5},{5,4},{6,7},{7,6},{8,9},{9,8},{10,11... | collective-permute-start | bytes 3145736 | tf_op jit(solution)/shard_map/ppermute | solution.py:166
  439.2 57.1 %all-to-all-start.7 = ((bf16[16,256,128]{2,1,0:T(8,128)(2,1)}), bf16[16,256,128]{2,1,0:T(8,128)(2,1)S(1)}, u32[]{:S(2)}, u32[]{:S(2)}) async-start(bf16[16,256,128]{2,1,0:T(8,128)(2,1)} %bitcast.63), calls=%async_computation.8 | async-start | bytes 2097152 | tf_op jit(solution)/shard_map/all_to_all | solution.py:163
  445.2 35.2 %copy-start.10 = (f32[4096,256]{1,0:T(8,128)S(1)}, f32[4096,256]{1,0:T(8,128)}, u32[]{:S(2)}) copy-start(f32[4096,256]{1,0:T(8,128)} %copy-done.9) | copy-start | bytes 12582916
  496.3 53.9 %all-to-all-start.6 = ((bf16[16,256,128]{2,1,0:T(8,128)(2,1)}), bf16[16,256,128]{2,1,0:T(8,128)(2,1)S(1)}, u32[]{:S(2)}, u32[]{:S(2)}) async-start(bf16[16,256,128]{2,1,0:T(8,128)(2,1)} %bitcast.46), calls=%async_computation.7 | async-start | bytes 2097152 | tf_op jit(solution)/shard_map/all_to_all | solution.py:163
  550.2 30.6 %all-to-all-start.5 = ((bf16[16,256,128]{2,1,0:T(8,128)(2,1)}), bf16[16,256,128]{2,1,0:T(8,128)(2,1)S(1)}, u32[]{:S(2)}, u32[]{:S(2)}) async-start(bf16[16,256,128]{2,1,0:T(8,128)(2,1)} %bitcast.302), calls=%async_computation.6 | async-start | bytes 2097152 | tf_op jit(solution)/shard_map/all_to_all | solution.py:163
  637.7 13.7 %collective-permute-start.4 = (bf16[128,2048]{1,0:T(8,128)(2,1)S(1)}, bf16[128,2048]{1,0:T(8,128)(2,1)S(1)}, u32[]{:S(2)}, u32[]{:S(2)}) collective-permute-start(bf16[128,2048]{1,0:T(8,128)(2,1)S(1)} %get-tuple-element.5), channel_id=1, source_target_pairs={{0,1},{1,0},{2,3},{3,2},{4,5},{5,4},{6,7},{7,6},{8,9},{9,8},{10,11... | collective-permute-start | bytes 1572872 | tf_op jit(solution)/shard_map/ppermute | solution.py:166
  644.8 7.8 %copy-start.1 = (bf16[2,128,4096]{2,1,0:T(8,128)(2,1)S(1)}, bf16[2,128,4096]{2,1,0:T(8,128)(2,1)}, u32[]{:S(2)}) copy-start(bf16[2,128,4096]{2,1,0:T(8,128)(2,1)} %param.7) | copy-start | bytes 6291460
Sparse Core Ops, SparseCore 0:
  10.7 185.1 all-gather.1
  402.3 234.0 reduce-scatter.1

commit v2 on v1

--- a/solution.py
+++ b/solution.py
@@ -1,9 +1,15 @@
+import functools
 import math
 
 import jax
 import jax.numpy as jnp
 from jax import lax
+from jax.experimental import pallas as pl
+from jax.experimental.pallas import tpu as pltpu
 from jax.sharding import Mesh, PartitionSpec as P
+
+MESH = pl.DeviceIdType.MESH
+ANY = pl.BlockSpec(memory_space=pl.ANY)
 
 HD = 128
 
@@ -135,6 +141,298 @@
     return body
 
 
+def greet(peers):
+    barrier = pltpu.get_barrier_semaphore()
+    for peer in peers:
+        pl.semaphore_signal(barrier, inc=1, device_id=peer, device_id_type=MESH)
+    pl.semaphore_wait(barrier, len(peers))
+
+
+def place(n_frame):
+    me, side = lax.axis_index("frame"), lax.axis_index("head")
+    z, x, c = me // 4, (me // 2) % 2, me % 2
+    peers = [(lax.rem(me + j, n_frame), side) for j in range(1, n_frame)] + [(me, 1 - side)]
+    return me, side, z, x, c, peers
+
+
+def gather_kernel(n_frame, acts, cot, wq, wk, wv, acts_all, w_all, cot_all, cot_far, *sems):
+    send_z, recv_z, send_x, recv_x, send_c, recv_c = sems[:6]
+    send_w, recv_w, send_y, recv_y, send_t, recv_t, local = sems[6:]
+    n_z = n_frame // 4
+    me, side, z, x, c, peers = place(n_frame)
+    rows = wq.shape[0]
+    toks = acts.shape[0]
+    weights = (wq, wk, wv)
+
+    def index(zz, xx, cc):
+        return (zz * 2 + xx) * 2 + cc
+
+    def remote(src, dst, send, recv, to):
+        return pltpu.make_async_remote_copy(
+            src_ref=src, dst_ref=dst, send_sem=send, recv_sem=recv, device_id=to, device_id_type=MESH
+        )
+
+    def w_rows(f, part, width):
+        return w_all.at[pl.ds(pl.multiple_of(f * rows, rows), rows), pl.ds(part, width)]
+
+    def t_rows(f, part):
+        return cot_all.at[pl.ds(pl.multiple_of(f * toks, toks), toks), pl.ds(part * HD, HD)]
+
+    def w_from(src):
+        f = pl.multiple_of(src * HD, HD)
+        return [w.at[:, pl.ds(f, HD)] for w in weights]
+
+    def a_from(zz, xx, cc, own=False):
+        return acts if own else acts_all.at[index(zz, xx, cc)]
+
+    greet(peers)
+    partner = (me, 1 - side)
+    far = remote(cot.at[1], cot_far, send_t.at[0], recv_t.at[0], partner)
+    far.start()
+
+    def hop(way, step):
+        step_z = 2 * way - 1
+        block = z - step_z * (step - 1)
+        src = acts if step == 1 else acts_all.at[index(block, x, c)]
+        valid = (z + 1 < n_z) if way else (z >= 1)
+        if step > 1:
+            valid = valid & ((block >= 0) if way else (block < n_z))
+        at = way * (n_z - 1) + step - 1
+        to = (index(z + step_z, x, c), side)
+        return valid, lambda: remote(src, acts_all.at[index(block, x, c)], send_z.at[at], recv_z.at[at], to)
+
+    def landed(way, step):
+        step_z = 2 * way - 1
+        block = z - step_z * step
+        valid = (block >= 0) if way else (block < n_z)
+        at = way * (n_z - 1) + step - 1
+        return valid, block, lambda: remote(
+            acts, acts_all.at[index(block, x, c)], send_z.at[at], recv_z.at[at], (me, 1 - side)
+        )
+
+    def beside(slot, block, own=False):
+        return remote(
+            a_from(block, x, c, own), acts_all.at[index(block, x, c)],
+            send_x.at[slot], recv_x.at[slot], (index(z, 1 - x, c), side),
+        )
+
+    def over(slot, block, xx, own=False):
+        return remote(
+            a_from(block, xx, c, own), acts_all.at[index(block, xx, c)],
+            send_c.at[slot], recv_c.at[slot], (index(z, x, 1 - c), side),
+        )
+
+    def slot_of(block):
+        return lax.rem(block - z + n_z, n_z)
+
+    def send_weights(j):
+        to = lax.rem(me + j, n_frame)
+        for i, src in enumerate(w_from(to)):
+            remote(src, w_rows(me, i * HD, HD), send_w.at[j, i], recv_w.at[j, i], (to, side)).start()
+        remote(cot.at[0, to], t_rows(me, 0), send_t.at[j], recv_t.at[j], (to, side)).start()
+
+    for way in range(2):
+        valid, make = hop(way, 1)
+        pl.when(valid)(lambda make=make: make().start())
+    beside(0, z, True).start()
+    over(0, z, x, True).start()
+
+    keep = [pltpu.make_async_copy(acts, acts_all.at[me], local.at[0])]
+    for i, src in enumerate(w_from(me)):
+        keep.append(pltpu.make_async_copy(src, w_rows(me, i * HD, HD), local.at[1 + i]))
+    keep.append(pltpu.make_async_copy(cot.at[0, me], t_rows(me, 0), local.at[4]))
+    for copy in keep:
+        copy.start()
+
+    third = (n_frame - 1 + 2) // 3
+    order = []
+    for j in range(1, n_frame // 2 + 1):
+        order.append(j)
+        if j != n_frame - j:
+            order.append(n_frame - j)
+    batches = [order[i * third : (i + 1) * third] for i in range(3)]
+    for j in batches[0]:
+        send_weights(j)
+    for step in range(1, n_z):
+        for way in range(2):
+            valid, block, make = landed(way, step)
+
+            def pass_on(way=way, step=step, block=block, make=make):
+                make().wait_recv()
+                if step + 1 < n_z:
+                    more, again = hop(way, step + 1)
+                    pl.when(more)(lambda: again().start())
+                beside(slot_of(block), block).start()
+                over(slot_of(block), block, x).start()
+
+            pl.when(valid)(pass_on)
+        for j in batches[step] if step < 3 else ():
+            send_weights(j)
+    for batch in batches[n_z:] if n_z < 3 else ():
+        for j in batch:
+            send_weights(j)
+
+    far.wait_recv()
+    for j in range(1, n_frame):
+        to = lax.rem(me + j, n_frame)
+        remote(
+            cot_far.at[to], t_rows(me, 1), send_t.at[n_frame + j - 1], recv_t.at[n_frame + j - 1], (to, side)
+        ).start()
+    kept_far = pltpu.make_async_copy(cot_far.at[me], t_rows(me, 1), local.at[5])
+    kept_far.start()
+
+    for copy in keep:
+        copy.wait()
+
+    def share(j):
+        f = lax.rem(me + n_frame - j, n_frame)
+        return remote(
+            w_rows(f, 0, 3 * HD), w_rows(f, 3 * HD, 3 * HD), send_y.at[j], recv_y.at[j], partner
+        )
+
+    share(0).start()
+    for j in order:
+        f = lax.rem(me + n_frame - j, n_frame)
+        for i, src in enumerate(w_from(f)):
+            remote(src, w_rows(f, i * HD, HD), send_w.at[j, i], recv_w.at[j, i], partner).wait_recv()
+        share(j).start()
+
+    for slot in range(n_z):
+        block = lax.rem(z + slot, n_z)
+        remote(
+            acts, acts_all.at[index(block, 1 - x, c)], send_x.at[slot], recv_x.at[slot], partner
+        ).wait_recv()
+        over(n_z + slot, block, 1 - x).start()
+    for slot in range(n_z):
+        block = lax.rem(z + slot, n_z)
+        for group, xx in ((0, x), (n_z, 1 - x)):
+            remote(
+                acts, acts_all.at[index(block, xx, 1 - c)],
+                send_c.at[group + slot], recv_c.at[group + slot], partner,
+            ).wait_recv()
+    for j in range(n_frame):
+        share(j).wait_recv()
+        share(j).wait_send()
+    for j in range(1, n_frame):
+        f = lax.rem(me + n_frame - j, n_frame)
+        for part, at in ((0, j), (1, n_frame + j - 1)):
+            copy = remote(cot.at[0, f], t_rows(f, part), send_t.at[at], recv_t.at[at], partner)
+            copy.wait_recv()
+            copy.wait_send()
+        for i, src in enumerate(w_from(f)):
+            remote(src, w_rows(f, i * HD, HD), send_w.at[j, i], recv_w.at[j, i], partner).wait_send()
+    far.wait_send()
+    kept_far.wait()
+    for way in range(2):
+        for step in range(1, n_z):
+            valid, make = hop(way, step)
+            pl.when(valid)(lambda make=make: make().wait_send())
+    for slot in range(n_z):
+        block = lax.rem(z + slot, n_z)
+        beside(slot, block, slot == 0).wait_send()
+        over(slot, block, x, slot == 0).wait_send()
+        over(n_z + slot, block, 1 - x).wait_send()
+
+
+def gather_all(n_frame, acts, cot, wq, wk, wv):
+    toks, width = acts.shape
+    n_z = n_frame // 4
+    dma = pltpu.SemaphoreType.DMA
+    bf16 = jnp.bfloat16
+    out = pl.pallas_call(
+        functools.partial(gather_kernel, n_frame),
+        out_shape=(
+            jax.ShapeDtypeStruct((n_frame, toks, width), bf16),
+            jax.ShapeDtypeStruct((width, 6 * HD), bf16),
+            jax.ShapeDtypeStruct((n_frame * toks, 2 * HD), bf16),
+            jax.ShapeDtypeStruct((n_frame, toks, HD), bf16),
+        ),
+        in_specs=[ANY] * 5,
+        out_specs=(ANY,) * 4,
+        scratch_shapes=[
+            dma((2 * (n_z - 1),)), dma((2 * (n_z - 1),)),
+            dma((n_z,)), dma((n_z,)),
+            dma((2 * n_z,)), dma((2 * n_z,)),
+            dma((n_frame, 3)), dma((n_frame, 3)),
+            dma((n_frame,)), dma((n_frame,)),
+            dma((2 * n_frame,)), dma((2 * n_frame,)),
+            dma((6,)),
+        ],
+        compiler_params=pltpu.CompilerParams(collective_id=0, has_side_effects=True),
+        name="gather_all",
+    )(acts, cot, wq, wk, wv)
+    return out[:3]
+
+
+def attention_kernel(raw, cot, q_gain, k_gain, out):
+    frames, some, _ = raw.shape
+    n = frames * some
+
+    def flat(x):
+        return x.astype(jnp.float32).reshape(n, HD)
+
+    def put(part, x):
+        out[:, :, part * HD : (part + 1) * HD] = x.reshape(frames, some, HD).astype(out.dtype)
+
+    def normed(x, gain):
+        inverse = lax.rsqrt(jnp.mean(x * x, axis=-1, keepdims=True) + epsilon)
+        return inverse, (x * inverse * gain).astype(jnp.bfloat16)
+
+    def pulled(x, inverse, gain, d):
+        d = d.astype(jnp.bfloat16).astype(jnp.float32) * gain
+        along = jnp.sum(x * d, axis=-1, keepdims=True) * (1.0 / HD)
+        return inverse * d - x * (inverse * inverse * inverse * along)
+
+    def dot(a, b, ca, cb):
+        return lax.dot_general(
+            a, b, (((ca,), (cb,)), ((), ())), preferred_element_type=jnp.float32
+        )
+
+    q, k = flat(raw[:, :, :HD]), flat(raw[:, :, HD : 2 * HD])
+    v = flat(raw[:, :, 2 * HD :]).astype(jnp.bfloat16)
+    g = flat(cot[...]).astype(jnp.bfloat16)
+    gq, gk = q_gain[...], k_gain[...]
+    iq, qn = normed(q, gq)
+    ik, kn = normed(k, gk)
+    factor = 1.0 / math.sqrt(HD)
+    row = lax.broadcasted_iota(jnp.int32, (n, n), 0)
+    col = lax.broadcasted_iota(jnp.int32, (n, n), 1)
+    same = lax.rem(row, some) == lax.rem(col, some)
+    expon = jnp.where(same, jnp.exp(dot(qn, kn, 1, 1) * factor), 0.0)
+    prob = expon / jnp.sum(expon, axis=-1, keepdims=True)
+    d_prob = dot(g, v, 1, 1)
+    mean = jnp.sum(prob * d_prob, axis=-1, keepdims=True)
+    d_scores = (prob * (d_prob - mean) * factor).astype(jnp.bfloat16)
+    put(2, dot(prob.astype(jnp.bfloat16), g, 0, 0))
+    put(0, pulled(q, iq, gq, dot(d_scores, kn, 1, 0)))
+    put(1, pulled(k, ik, gk, dot(d_scores, qn, 0, 0)))
+
+
+def attention_back(raw, cot, q_gain, k_gain, frames):
+    half = raw.shape[0] // frames
+    heads = cot.shape[1] // HD
+    some = 8
+    return pl.pallas_call(
+        attention_kernel,
+        grid=(half // some, heads),
+        out_shape=jax.ShapeDtypeStruct((frames, half, raw.shape[1]), jnp.bfloat16),
+        in_specs=[
+            pl.BlockSpec((frames, some, 3 * HD), lambda p, h: (0, p, h)),
+            pl.BlockSpec((frames, some, HD), lambda p, h: (0, p, h)),
+            pl.BlockSpec((1, HD), lambda p, h: (0, 0)),
+            pl.BlockSpec((1, HD), lambda p, h: (0, 0)),
+        ],
+        out_specs=pl.BlockSpec((frames, some, 3 * HD), lambda p, h: (0, p, h)),
+        compiler_params=pltpu.CompilerParams(dimension_semantics=("arbitrary", "arbitrary")),
+        name="attention_back",
+    )(
+        raw.reshape(frames, half, -1),
+        cot.reshape(frames, half, -1),
+        q_gain.reshape(1, HD),
+        k_gain.reshape(1, HD),
+    ).reshape(frames * half, -1)
+
+
 def make_patch_body(n_frame):
     swap = [(0, 1), (1, 0)]
 
@@ -142,9 +440,7 @@
         frames_here, patches, width = activations.shape
         rows_here, head_cols = w_query.shape
         half = patches // 2
-        cols = head_cols // n_frame
         frames = frames_here * n_frame
-        tokens = frames * half
         side = lax.axis_index("head")
 
         def halves(x, axis, size):
@@ -159,53 +455,26 @@
                 jnp.concatenate([other, mine], axis),
             )
 
-        def exchange(x):
-            return lax.all_to_all(x, "frame", split_axis=0, concat_axis=0, tiled=True)
-
         def across(x):
             return lax.ppermute(x, "head", swap)
 
         def by_head(x):
-            return jnp.concatenate([x[:, i * cols : (i + 1) * cols] for i in range(n_frame)], axis=0)
+            return x.reshape(-1, n_frame, HD).transpose(1, 0, 2)
 
         own_acts, _ = halves(activations, 1, half)
-        acts = lax.all_gather(own_acts.reshape(-1, width), "frame", axis=0, tiled=True)
-
-        cot_mine, cot_other = halves(grad_attn, 1, half)
-        cot_other = across(cot_other)
-        mine = [exchange(by_head(w)) for w in (w_query, w_key, w_value)]
-        wq, wk, wv = (jnp.concatenate([w, across(w)], axis=1) for w in mine)
-        cotan = jnp.concatenate(
-            [
-                exchange(by_head(x.reshape(-1, head_cols)))
-                for x in (cot_mine, cot_other)
-            ],
-            axis=1,
-        )
-
-        heads = 2 * cols // HD
-        shape4 = (frames, half, heads, HD)
-        shape3 = (tokens, heads, HD)
-        q_raw = jnp.dot(acts, wq, preferred_element_type=jnp.float32).reshape(shape3)
-        k_raw = jnp.dot(acts, wk, preferred_element_type=jnp.float32).reshape(shape3)
-        value = jnp.dot(acts, wv, preferred_element_type=jnp.float32)
-        value = value.astype(jnp.bfloat16).reshape(shape4)
-        q_norm = scaled(q_raw, q_gain).astype(jnp.bfloat16).reshape(shape4)
-        k_norm = scaled(k_raw, k_gain).astype(jnp.bfloat16).reshape(shape4)
-        d_qn, d_kn, d_val = attend_back(q_norm, k_norm, value, cotan.reshape(shape4))
-
-        _, pull_query = jax.vjp(lambda raw: scaled(raw, q_gain), q_raw)
-        _, pull_key = jax.vjp(lambda raw: scaled(raw, k_gain), k_raw)
-        d_q = pull_query(d_qn.reshape(shape3).astype(jnp.float32))[0]
-        d_q = d_q.astype(jnp.bfloat16).reshape(tokens, 2 * cols)
-        d_k = pull_key(d_kn.reshape(shape3).astype(jnp.float32))[0]
-        d_k = d_k.astype(jnp.bfloat16).reshape(tokens, 2 * cols)
-        d_v = d_val.reshape(tokens, 2 * cols)
-
-        d_all = jnp.concatenate([d_q, d_k, d_v], axis=1)
-        w_all = jnp.concatenate([wq, wk, wv], axis=1)
+        cot = jnp.stack([by_head(x) for x in halves(grad_attn, 1, half)])
+        acts, w_all, cotan = gather_all(
+            n_frame, own_acts.reshape(-1, width), cot, w_query, w_key, w_value
+        )
+        acts = acts.reshape(-1, width)
+        raw = jnp.dot(acts, w_all, preferred_element_type=jnp.float32)
+        d_all = attention_back(raw, cotan, q_gain, k_gain, frames)
+
         partial = lax.dot_general(
             d_all, w_all, (((1,), (1,)), ((), ())), preferred_element_type=jnp.float32
+        ).astype(jnp.bfloat16)
+        terms = lax.dot_general(
+            acts, d_all, (((0,), (0,)), ((), ())), preferred_element_type=jnp.float32
         ).astype(jnp.bfloat16)
         partial = lax.psum_scatter(partial, "frame", scatter_dimension=0, tiled=True)
         mine_cols, other_cols = halves(partial, 1, head_cols)
@@ -213,17 +482,16 @@
         grad_input = rejoin(
             mine_cols.reshape(shape_out), across(other_cols).reshape(shape_out), 1
         )
-
-        def weight_grad(d):
-            term = lax.dot_general(
-                acts, d, (((0,), (0,)), ((), ())), preferred_element_type=jnp.float32
-            )
-            total = term[:, :cols] + across(term[:, cols:].astype(jnp.bfloat16)).astype(jnp.float32)
-            out = exchange(total.astype(jnp.bfloat16))
-            out = [out[i * rows_here : (i + 1) * rows_here] for i in range(n_frame)]
-            return jnp.concatenate(out, axis=1).astype(jnp.float32)
-
-        return (grad_input, weight_grad(d_q), weight_grad(d_k), weight_grad(d_v))
+        cols = 3 * HD
+        near = terms[:, :cols].astype(jnp.float32) + across(terms[:, cols:]).astype(jnp.float32)
+        near = near.astype(jnp.bfloat16)
+        near = lax.all_to_all(near, "frame", split_axis=0, concat_axis=0, tiled=True)
+        near = near.reshape(n_frame, rows_here, 3, HD)
+        grads = [
+            near[:, :, i].transpose(1, 0, 2).reshape(rows_here, head_cols).astype(jnp.float32)
+            for i in range(3)
+        ]
+        return (grad_input, *grads)
 
     return body
 
@@ -251,7 +519,12 @@
 
     def run(activations, w_query, w_key, w_value, q_gain, k_gain, grad_attn):
         heads_here = w_query.shape[1] // (HD * n_head)
-        if n_head == 2 and heads_here % n_frame == 0 and activations.shape[1] % n_head == 0:
+        if (
+            n_head == 2
+            and heads_here == n_frame
+            and n_frame % 4 == 0
+            and activations.shape[1] % (8 * n_head) == 0
+        ):
             return by_patch(activations, w_query, w_key, w_value, q_gain, k_gain, grad_attn)
         n_a = line_split(n_frame, w_query.shape[1] // (HD * n_head))
         n_b = n_frame // n_a

time: 673 us -> 525 us (0.78); the launches traced: 660 us -> 520 us
  Pallas kernels: 0 us -> 177 us
  local copies, waits for them, and re-layouts: 165 us -> 18.4 us
  waiting for transfers between devices: 304 us -> 182 us
  matrix products: 91.8 us -> 56.8 us
  other arithmetic: 30.1 us -> 7.46 us
  starting transfers between devices: 54.3 us -> 64.6 us
    all_to_all x8 -> x1, waiting for transfers between devices: 186 us -> 0.01 us  [body(): lax.all_to_all(near, 'frame', split_axis=0, concat_axis=0, tiled=True)]
    pallas_call x0 -> x2, Pallas kernels: none -> 177 us  [the longest x1 160 us: gather_all(): pl.pallas_call(functools.partial(gather_kernel, n_frame), out_shape=(jax....]
    unnamed x168 -> x15, local copies, waits for them, and re-layouts: 97.8 us -> 10.2 us
    reduce_scatter x1, waiting for transfers between devices: 47.3 us -> 111 us  [body(): lax.psum_scatter(partial, 'frame', scatter_dimension=0, tiled=True)]
    dot_general x11 -> x2, matrix products: 72.6 us -> 37.1 us  [the longest x1 19.9 us: body(): raw = jnp.dot(acts, w_all, preferred_element_type=jnp.float32)]
    convert_element_type x7 -> x0, local copies, waits for them, and re-layouts: 30.4 us -> none  [the longest x3 14.8 us: body(): d_k = pull_key(d_kn.reshape(shape3).astype(jnp.float32))[0]]
    reshape x9 -> x0, local copies, waits for them, and re-layouts: 26.5 us -> none  [the longest x3 12.3 us: body(): jnp.dot(acts, wk, preferred_element_type=jnp.float32).reshape(shape3)]
    all_to_all x8 -> x1, starting transfers between devices: 43.2 us -> 62 us  [body(): lax.all_to_all(near, 'frame', split_axis=0, concat_axis=0, tiled=True)]
  transfers between devices with their start and end apart: 18 -> 4, of which waited for: 13 -> 3; matrix products, arithmetic and copies ran while one was open for 22% -> 7% of each run, Pallas kernels for 0% -> 0%
where the time goes in v2:
time: 525 us; the launch traced here: 520 us
  waiting for transfers between devices  182 us (35%)
  Pallas kernels  177 us (34%)
  starting transfers between devices  64.6 us (12%)
  matrix products  56.8 us (11%)
  local copies, waits for them, and re-layouts  18.4 us (4%)
  between operations  14.1 us (3%)
  other arithmetic  7.46 us (1%)
    pallas_call x1, Pallas kernels, gather_all(): pl.pallas_call(functools.partial(gather_kernel, n_frame), out_shape=(jax....  160 us
    reduce_scatter x1, waiting for transfers between devices, body(): lax.psum_scatter(partial, 'frame', scatter_dimension=0, tiled=True)  111 us
    ppermute x2, waiting for transfers between devices, across(): return lax.ppermute(x, 'head', swap)  70.8 us
    all_to_all x1, starting transfers between devices, body(): lax.all_to_all(near, 'frame', split_axis=0, concat_axis=0, tiled=True)  62 us
    dot_general x1, matrix products, body(): raw = jnp.dot(acts, w_all, preferred_element_type=jnp.float32)  19.9 us
    dot_general x1, matrix products, body(): lax.dot_general(d_all, w_all, (((1,), (1,)), ((), ())), preferred_element...  19.7 us
    dot_general x1, matrix products, body(): lax.dot_general(acts, d_all, (((0,), (0,)), ((), ())), preferred_element_...  17.2 us
    pallas_call x1, Pallas kernels, attention_back(): pl.pallas_call(attention_kernel, grid=(half // some, heads), out_shape=ja...  17.1 us
  transfers between devices with their start and end apart: 4, of which 3 were waited for; matrix products, arithmetic and copies ran while one was open for 7% of the time, Pallas kernels for 0%

profile of v2, /device:TPU:16, one launch (start us, length us, event | category | flops | bytes accessed | tf_op | source)
XLA Modules:
  0.0 520.2 jit_solution(6332297123071406749)
XLA Ops:
  7.2 0.0 copy-start
  7.2 0.0 reduce-scatter.2.cloned.1.call-start
  7.2 1.4 constant_dynamic-slice_fusion.3
  8.7 0.1 copy.20
  8.8 0.1 copy.21
  8.9 0.2 copy-done
  9.1 1.0 constant_dynamic-slice_fusion.4
  10.1 0.3 copy_bitcast_fusion
  10.4 1.1 pad_maximum_fusion.cot
  11.5 159.9 %gather_all.1 = (bf16[16,128,4096]{2,1,0:T(8,128)(2,1)}, bf16[4096,768]{1,0:T(8,128)(2,1)}, bf16[2048,256]{1,0:T(8,128)(2,1)}, bf16[16,128,128]{2,1,0:T(8,128)(2,1)}) custom-call(bf16[128,4096]{1,0:T(8,128)(2,1)} %bitcast.62, bf16[2,16,128,128]{3,2,1,0:T(8,128)(2,1)} %pad_maximum_fusion.cot, bf16[256,2048]{1,0:T(8,128)(2,1)} %wq.1, bf16[256,2048]{1,0:T(8,128)(2,1)} %wk.1, ...), custom_call_target="tpu_custom_call" | custom-call | tf_op jit(solution)/shard_map/gather_all/pallas_call | solution.py:342
  171.3 19.9 %fusion.raw = f32[32,64,768]{2,1,0:T(8,128)} fusion(bf16[32,64,4096]{2,1,0:T(8,128)(2,1)} %bitcast.73, bf16[4096,768]{1,0:T(8,128)(2,1)} %get-tuple-element.8), kind=kOutput, calls=%fused_computation.2 | convolution fusion | flops 12884901888 | bytes 29360128 | tf_op jit(solution)/shard_map/dot_general | solution.py:470
  191.2 17.1 %attention_back.1 = bf16[32,64,768]{2,1,0:T(8,128)(2,1)} custom-call(f32[32,64,768]{2,1,0:T(8,128)} %fusion.raw, bf16[32,64,256]{2,1,0:T(8,128)(2,1)} %bitcast.70, f32[1,128]{1,0:T(1,128)} %bitcast.71, f32[1,128]{1,0:T(1,128)} %bitcast.72), custom_call_target="tpu_custom_call" | custom-call | tf_op jit(solution)/shard_map/attention_back/pallas_call | solution.py:415
  208.3 19.7 %convolution_convert_fusion = bf16[2048,4096]{1,0:T(8,128)(2,1)} fusion(bf16[2048,768]{1,0:T(8,128)(2,1)} %bitcast.63, bf16[4096,768]{1,0:T(8,128)(2,1)} %get-tuple-element.8), kind=kOutput, calls=%fused_computation | convolution fusion | flops 12893290496 | bytes 26214400 | tf_op jit(solution)/shard_map/dot_general | solution.py:473
  228.0 0.0 copy-start.3
  228.0 0.0 reduce-scatter.2.cloned.1.call-update
  228.0 1.9 copy-done.3
  229.8 17.2 %convolution_convert_fusion.1 = bf16[4096,768]{1,0:T(8,128)(2,1)S(1)} fusion(bf16[2048,4096]{1,0:T(8,128)(2,1)} %bitcast.74, bf16[2048,768]{1,0:T(8,128)(2,1)S(1)} %bitcast.64), kind=kOutput, calls=%fused_computation.1 | convolution fusion | flops 12888047616 | bytes 26214400 | tf_op jit(solution)/shard_map/dot_general | solution.py:476
  247.1 0.3 slice.21
  247.4 1.6 collective-permute-start.1
  249.0 68.6 %collective-permute-done.1 = bf16[4096,384]{1,0:T(8,128)(2,1)S(1)} collective-permute-done((bf16[4096,384]{1,0:T(8,128)(2,1)S(1)}, bf16[4096,384]{1,0:T(8,128)(2,1)S(1)}, u32[]{:S(2)}, u32[]{:S(2)}) %collective-permute-start.1) | collective-permute-done | bytes 3145760 | tf_op jit(solution)/shard_map/ppermute | solution.py:459
  317.6 0.9 add_convert_fusion
  318.5 2.9 copy.16
  321.4 62.0 %all-to-all-start = ((bf16[16,256,384]{1,2,0:T(8,128)(2,1)}), bf16[16,256,384]{1,2,0:T(8,128)(2,1)S(1)}, u32[]{:S(2)}, u32[]{:S(2)}) async-start(bf16[16,256,384]{1,2,0:T(8,128)(2,1)} %copy.16), calls=%async_computation.1 | async-start | bytes 6291456 | tf_op jit(solution)/shard_map/all_to_all | solution.py:488
  383.4 111.2 %reduce-scatter.2.cloned.1.call-done = bf16[128,4096]{1,0:T(8,128)(2,1)} async-done(((bf16[2048,4096]{1,0:T(8,128)(2,1)}), bf16[128,4096]{1,0:T(8,128)(2,1)}) %reduce-scatter.2.cloned.1.call-update) | async-done | bytes 1048592 | tf_op jit(solution)/shard_map/reduce_scatter | solution.py:479
  494.6 2.3 constant_dynamic-slice_fusion.1
  496.8 1.0 collective-permute-start
  497.9 0.0 all-to-all-done
  497.9 2.9 fusion.2
  500.8 0.0 copy-start.2
  500.8 3.0 copy.17
  503.8 0.0 copy-done.2
  503.8 1.8 copy.18
  505.6 0.0 copy-start.4
  505.6 0.0 copy-start.1
  505.6 3.0 copy.19
  508.7 2.1 collective-permute-done
  510.8 0.0 copy-done.4
  510.8 2.6 maximum_select_fusion
  513.4 0.0 copy-done.1
Async XLA Ops:
  7.2 1.9 copy-start
  7.2 487.4 %reduce-scatter.2.cloned.1.call-start = ((), (), s32[]{:S(2)}) async-start(), calls=%async_computation.2 | async-start | bytes 17825792 | tf_op jit(solution)/shard_map/reduce_scatter | solution.py:479
  228.0 1.9 copy-start.3
  247.4 70.2 %collective-permute-start.1 = (bf16[4096,384]{1,0:T(8,128)(2,1)S(1)}, bf16[4096,384]{1,0:T(8,128)(2,1)S(1)}, u32[]{:S(2)}, u32[]{:S(2)}) collective-permute-start(bf16[4096,384]{1,0:T(8,128)(2,1)S(1)} %slice.21), channel_id=1, source_target_pairs={{0,1},{1,0},{2,3},{3,2},{4,5},{5,4},{6,7},{7,6},{8,9},{9,8},{10,11... | collective-permute-start | bytes 9437192 | tf_op jit(solution)/shard_map/ppermute | solution.py:459
  321.4 176.4 %all-to-all-start = ((bf16[16,256,384]{1,2,0:T(8,128)(2,1)}), bf16[16,256,384]{1,2,0:T(8,128)(2,1)S(1)}, u32[]{:S(2)}, u32[]{:S(2)}) async-start(bf16[16,256,384]{1,2,0:T(8,128)(2,1)} %copy.16), calls=%async_computation.1 | async-start | bytes 6291456 | tf_op jit(solution)/shard_map/all_to_all | solution.py:488
  496.8 13.9 %collective-permute-start = (bf16[128,2048]{1,0:T(8,128)(2,1)}, bf16[128,2048]{1,0:T(8,128)(2,1)}, u32[]{:S(2)}, u32[]{:S(2)}) collective-permute-start(bf16[128,2048]{1,0:T(8,128)(2,1)} %get-tuple-element.18), channel_id=1, source_target_pairs={{0,1},{1,0},{2,3},{3,2},{4,5},{5,4},{6,7},{7,6},{8,9},{9,8},{10,11... | collective-permute-start | bytes 1572872 | tf_op jit(solution)/shard_map/ppermute | solution.py:459
  500.8 3.0 copy-start.2
  505.6 5.2 copy-start.4
  505.6 7.7 %copy-start.1 = (bf16[2,128,4096]{2,1,0:T(8,128)(2,1)S(1)}, bf16[2,128,4096]{2,1,0:T(8,128)(2,1)}, u32[]{:S(2)}) copy-start(bf16[2,128,4096]{2,1,0:T(8,128)(2,1)} %param.7) | copy-start | bytes 6291460
Sparse Core Ops, SparseCore 0:
  228.1 266.3 reduce-scatter.1
